TPU v7x, 32 devices: a whole 2x2x4 slice. The times are simulated.
32 devices in a mesh: rep: 2 (over x), blk: 16 (over z, y, core).
Axes of the slice: x: 2, y: 2, z: 4, core: 2. Of those that a mesh axis runs over, the one named last changes fastest.
Arguments:
- features: bfloat16 [4096, 512], P(('rep', 'blk')), may hold values from -6 to 6
- weight: bfloat16 [512, 512], replicated, may hold values from -0.25 to 0.25
- tile_values: bfloat16 [2, 16, 16, 2, 128, 128], P('rep', 'blk'), as said below
- tile_list: int32 [2, 16, 16, 2], P('rep', 'blk'), may hold values from -1 to 1, as said below
- train_mask: int32 [4096], P(('rep', 'blk')), may hold values 0 or 1
- cotangent: bfloat16 [4096, 512], P(('rep', 'blk')), may hold values from -6 to 6
Outputs:
- activated: bfloat16 [4096, 512], P(('rep', 'blk'))
- weight_grad: float32 [512, 512], replicated
- feature_grad: bfloat16 [4096, 512], P(('rep', 'blk'))
Inputs may be any that keep to these rules, and one draw needn't show every extreme that they name: `tile_list`: -1 marks an empty slot; 0 or 1 names the half h whose tile [r, b, j, h] is nonempty; the two slots of a pair never name the same half. The graph is undirected: block (u, v) of A is nonempty exactly when block (v, u) is, and every block (u, u) is nonempty. How many nonempty tiles a device holds differs from device to device. `tile_values`: the tile of block (u, v) is the transpose of the tile of block (v, u), so A is symmetric.
All inputs are finite; a program needn't handle non-finite values. No bound on the sum of `train_mask` on one device may be relied on, other than what follows from the above.
Results may differ from a plain program's by a relative error of at most 0.014.
Values may be sent and summed in bfloat16 or wider, within the bound.
A program may use at most 128 MiB of HBM per device.

v0:
```python
import math
import jax
import jax.numpy as jnp
from jax import lax
from jax.sharding import PartitionSpec as P

GELU_SCALE = math.sqrt(2.0 / math.pi)


def activation(pre_act):
    inner = GELU_SCALE * (pre_act + 0.044715 * pre_act * pre_act * pre_act)
    tanh_part = jnp.tanh(inner)
    act_value = 0.5 * pre_act * (1.0 + tanh_part)
    act_slope = 0.5 * (1.0 + tanh_part) + 0.5 * pre_act * (
        1.0 - tanh_part * tanh_part
    ) * GELU_SCALE * (1.0 + 3.0 * 0.044715 * pre_act * pre_act)
    return (act_value, act_slope)


def on_device(features, weight, tile_values, tile_list, train_mask, cotangent):
    tile_rows = features.shape[0]
    feat_width = features.shape[1]
    pair_list = tile_list[0, 0]
    presence = jnp.stack(
        [jnp.any(pair_list == 0, axis=1), jnp.any(pair_list == 1, axis=1)], axis=1
    ).astype(jnp.bfloat16)
    masked = tile_values[0, 0] * presence[:, :, None, None]
    projected = jnp.dot(features, weight, preferred_element_type=jnp.float32).astype(jnp.bfloat16)

    def apply_tiles(incoming):
        shard_count = incoming.shape[0] // tile_rows
        return jnp.einsum(
            "jhst,jtf->hsf",
            masked,
            incoming.reshape(shard_count, tile_rows, feat_width),
            preferred_element_type=jnp.float32,
        )

    partial_value = apply_tiles(lax.all_gather(projected, "blk", axis=0, tiled=True))
    summed = lax.psum_scatter(
        partial_value.reshape(2 * tile_rows, feat_width).astype(jnp.bfloat16),
        "rep",
        scatter_dimension=0,
        tiled=True,
    ).astype(jnp.float32)
    act_value, act_slope = activation(summed)
    activated = act_value.astype(jnp.bfloat16)
    grad_z = (
        cotangent.astype(jnp.float32) * train_mask.astype(jnp.float32)[:, None] * act_slope
    ).astype(jnp.bfloat16)
    folded = apply_tiles(lax.all_gather(grad_z, "blk", axis=0, tiled=True))
    prop_sums = lax.psum_scatter(
        folded.reshape(2 * tile_rows, feat_width).astype(jnp.bfloat16),
        "rep",
        scatter_dimension=0,
        tiled=True,
    )
    local_term = lax.dot_general(
        features, prop_sums, (((0,), (0,)), ((), ())), preferred_element_type=jnp.float32
    )
    weight_grad = lax.psum(local_term, ("rep", "blk"))
    feature_grad = lax.dot_general(
        prop_sums, weight, (((1,), (1,)), ((), ())), preferred_element_type=jnp.float32
    ).astype(jnp.bfloat16)
    return (activated, weight_grad, feature_grad)


def solution(mesh):
    in_specs = (
        P(("rep", "blk"), None),
        P(),
        P("rep", "blk", None, None, None, None),
        P("rep", "blk", None, None),
        P(("rep", "blk")),
        P(("rep", "blk"), None),
    )
    out_specs = (P(("rep", "blk"), None), P(), P(("rep", "blk"), None))
    return jax.shard_map(
        on_device, mesh=mesh, in_specs=in_specs, out_specs=out_specs, check_vma=False
    )
```

profile of v0, /device:TPU:0, one launch (start us, length us, event | category | flops | bytes accessed | tf_op | source)
XLA Modules:
  0.0 271.8 jit_solution(10915368503565097484)
XLA Ops:
  7.2 0.0 copy-start
  7.2 0.0 all-gather.3.cloned.1.call-start
  7.2 1.0 copy-done
  8.2 1.8 convolution_convert_fusion.1
  10.0 0.0 all-gather.3.cloned.1.call-update
  10.0 0.0 reduce-scatter.3.cloned.1.call-start
  10.1 0.7 compare_reduce_fusion.1
  10.8 0.1 copy.9
  10.9 1.4 bitcast_multiply_fusion
  12.3 0.0 copy-start.4
  12.3 0.0 copy-start.3
  12.3 42.6 %all-gather.3.cloned.1.call-done = bf16[2048,512]{1,0:T(8,128)(2,1)} async-done(((bf16[128,512]{1,0:T(8,128)(2,1)}), bf16[2048,512]{1,0:T(8,128)(2,1)}) %all-gather.3.cloned.1.call-update) | async-done | bytes 2097168 | tf_op jit(solution)/shard_map/all_gather | solution.py:39
  54.9 3.0 %fusion = bf16[256,512]{1,0:T(8,128)(2,1)} fusion(bf16[256,16,128]{2,0,1:T(8,128)(2,1)S(1)} %bitcast.29, bf16[16,128,512]{2,1,0:T(8,128)(2,1)} %bitcast.33), kind=kOutput, calls=%fused_computation.3 | convolution fusion | flops 537001984 | bytes 3407872 | tf_op jit(solution)/shard_map/jhst,jtf->hsf/dot_general | solution.py:32
  57.9 0.0 reduce-scatter.3.cloned.1.call-update
  58.0 0.0 all-gather.5.cloned.1.call-start
  58.0 0.0 copy-done.4
  58.0 10.6 %reduce-scatter.3.cloned.1.call-done = bf16[128,512]{1,0:T(8,128)(2,1)} async-done(((bf16[256,512]{1,0:T(8,128)(2,1)}), bf16[128,512]{1,0:T(8,128)(2,1)}) %reduce-scatter.3.cloned.1.call-update) | async-done | bytes 131088 | tf_op jit(solution)/shard_map/reduce_scatter | solution.py:40
  68.6 0.0 copy-done.3
  68.6 1.8 fusion.9
  70.4 0.0 all-gather.5.cloned.1.call-update
  70.4 0.0 reduce-scatter.5.cloned.1.call-start
  70.5 42.3 %all-gather.5.cloned.1.call-done = bf16[2048,512]{1,0:T(8,128)(2,1)} async-done(((bf16[128,512]{1,0:T(8,128)(2,1)}), bf16[2048,512]{1,0:T(8,128)(2,1)}) %all-gather.5.cloned.1.call-update) | async-done | bytes 2097168 | tf_op jit(solution)/shard_map/all_gather | solution.py:51
  112.8 3.0 %fusion.1 = bf16[256,512]{1,0:T(8,128)(2,1)} fusion(bf16[256,16,128]{2,0,1:T(8,128)(2,1)S(1)} %bitcast.30, bf16[16,128,512]{2,1,0:T(8,128)(2,1)} %bitcast.34), kind=kOutput, calls=%fused_computation.4 | convolution fusion | flops 537001984 | bytes 3407872 | tf_op jit(solution)/shard_map/jhst,jtf->hsf/dot_general | solution.py:32
  115.8 0.0 reduce-scatter.5.cloned.1.call-update
  115.8 0.0 all-reduce.2.cloned.1.call-start
  115.9 10.6 %reduce-scatter.5.cloned.1.call-done = bf16[128,512]{1,0:T(8,128)(2,1)} async-done(((bf16[256,512]{1,0:T(8,128)(2,1)}), bf16[128,512]{1,0:T(8,128)(2,1)}) %reduce-scatter.5.cloned.1.call-update) | async-done | bytes 131088 | tf_op jit(solution)/shard_map/reduce_scatter | solution.py:52
  126.5 0.0 copy-done.1
  126.5 2.3 convolution_bitcast_fusion
  128.8 0.0 all-reduce.2.cloned.1.call-update
  128.8 1.0 convolution_convert_fusion
  129.7 133.0 %all-reduce.2.cloned.1.call-done = f32[512,512]{0,1:T(8,128)} async-done(((f32[512,512]{0,1:T(8,128)}), f32[512,512]{0,1:T(8,128)}) %all-reduce.2.cloned.1.call-update) | async-done | bytes 1048592 | tf_op jit(solution)/shard_map/psum | solution.py:61
  262.7 2.5 copy.10
  (5 shorter events, 0.0 us)
Async XLA Ops:
  7.2 1.0 copy-start
  7.2 47.8 %all-gather.3.cloned.1.call-start = ((), (), s32[]{:S(2)}) async-start(), calls=%async_computation.2 | async-start | bytes 2228224 | tf_op jit(solution)/shard_map/all_gather | solution.py:39
  10.0 58.6 %reduce-scatter.3.cloned.1.call-start = ((), (), s32[]{:S(2)}) async-start(), calls=%async_computation.3 | async-start | bytes 393216 | tf_op jit(solution)/shard_map/reduce_scatter | solution.py:40
  12.3 45.8 %copy-start.4 = (s32[128]{0:T(128)S(1)}, s32[128]{0:T(128)}, u32[]{:S(2)}) copy-start(s32[128]{0:T(128)} %param.10) | copy-start | bytes 1540
  12.3 56.3 %copy-start.3 = (bf16[128,512]{1,0:T(8,128)(2,1)S(1)}, bf16[128,512]{1,0:T(8,128)(2,1)}, u32[]{:S(2)}) copy-start(bf16[128,512]{1,0:T(8,128)(2,1)} %param.11) | copy-start | bytes 393220
  58.0 54.9 %all-gather.5.cloned.1.call-start = ((), (), s32[]{:S(2)}) async-start(), calls=%async_computation.4 | async-start | bytes 2228224 | tf_op jit(solution)/shard_map/all_gather | solution.py:51
  70.4 56.1 %copy-start.1 = (bf16[128,512]{1,0:T(8,128)(2,1)S(1)}, bf16[128,512]{1,0:T(8,128)(2,1)}, u32[]{:S(2)}) copy-start(bf16[128,512]{1,0:T(8,128)(2,1)} %param.6) | copy-start | bytes 393220
  70.4 56.0 %reduce-scatter.5.cloned.1.call-start = ((), (), s32[]{:S(2)}) async-start(), calls=%async_computation.5 | async-start | bytes 393216 | tf_op jit(solution)/shard_map/reduce_scatter | solution.py:52
  115.8 146.9 %all-reduce.2.cloned.1.call-start = ((), (), s32[]{:S(2)}) async-start(), calls=%async_computation.6 | async-start | bytes 2097152 | tf_op jit(solution)/shard_map/psum | solution.py:61
  126.5 2.3 copy-start.2
Sparse Core Ops, SparseCore 0:
  10.7 44.1 all-gather.2
  58.1 10.4 reduce-scatter.2
  71.3 41.4 all-gather.4
  116.0 10.4 reduce-scatter.4
  132.1 130.6 all-reduce.1
where the time goes:
time: 272 us
  waiting for transfers between devices  239 us (88%)
  between operations  13.8 us (5%)
  matrix products  11 us (4%)
  other arithmetic  3.89 us (1%)
  local copies, waits for them, and re-layouts  3.64 us (1%)
    psum x1, waiting for transfers between devices, on_device(): weight_grad = lax.psum(local_term, ('rep', 'blk'))  133 us
    all_gather x1, waiting for transfers between devices, on_device(): lax.all_gather(projected, 'blk', axis=0, tiled=True)  42.6 us
    all_gather x1, waiting for transfers between devices, on_device(): folded = apply_tiles(lax.all_gather(grad_z, 'blk', axis=0, tiled=True))  42.3 us
    reduce_scatter x1, waiting for transfers between devices, on_device(): lax.psum_scatter(folded.reshape(2 * tile_rows, feat_width).astype(jnp.bfl...  10.6 us
    reduce_scatter x1, waiting for transfers between devices, on_device(): lax.psum_scatter(partial_value.reshape(2 * tile_rows, feat_width).astype(...  10.6 us
    dot_general x2, matrix products, apply_tiles(): jnp.einsum('jhst,jtf->hsf', masked, incoming.reshape(shard_count, tile_ro...  6 us
  transfers between devices with their start and end apart: 5, of which 5 were waited for; matrix products, arithmetic and copies ran while one was open for 1% of the time, Pallas kernels for 0%

commit v1 on v0

--- a/solution.py
+++ b/solution.py
@@ -5,6 +5,20 @@
 from jax.sharding import PartitionSpec as P
 
 GELU_SCALE = math.sqrt(2.0 / math.pi)
+
+
+def rest_edge(own_rows):
+    local_part = lax.axis_size("blk")
+    z2 = lax.axis_index("blk")
+    u_next, mixed_arr = (local_part, z2)
+    big, frame_out = (own_rows, 1)
+    while frame_out < u_next:
+        local_out = lax.ppermute(big, "blk", [(w, w ^ frame_out) for w in range(u_next)])
+        found_now = jnp.concatenate([big, local_out], axis=0)
+        then = jnp.concatenate([local_out, big], axis=0)
+        big = jnp.where(mixed_arr & frame_out == 0, found_now, then)
+        frame_out = 2 * frame_out
+    return big
 
 
 def activation(pre_act):
@@ -48,7 +62,7 @@
     grad_z = (
         cotangent.astype(jnp.float32) * train_mask.astype(jnp.float32)[:, None] * act_slope
     ).astype(jnp.bfloat16)
-    folded = apply_tiles(lax.all_gather(grad_z, "blk", axis=0, tiled=True))
+    folded = apply_tiles(rest_edge(grad_z))
     prop_sums = lax.psum_scatter(
         folded.reshape(2 * tile_rows, feat_width).astype(jnp.bfloat16),
         "rep",

time: 272 us -> 301 us (1.11)
  waiting for transfers between devices: 239 us -> 263 us
  starting transfers between devices: 0.21 us -> 5.69 us
    ppermute x0 -> x4, waiting for transfers between devices: none -> 64.4 us  [rest_edge(): lax.ppermute(big, 'blk', [(w, w ^ frame_out) for w in range(u_next)])]
    all_gather x1 -> x0, waiting for transfers between devices: 42.3 us -> none  [on_device(): folded = apply_tiles(lax.all_gather(grad_z, 'blk', axis=0, tiled=True))]
    ppermute x0 -> x4, starting transfers between devices: none -> 5.53 us  [rest_edge(): lax.ppermute(big, 'blk', [(w, w ^ frame_out) for w in range(u_next)])]
  transfers between devices with their start and end apart: 5 -> 8, of which waited for: 5 -> 8; matrix products, arithmetic and copies ran while one was open for 1% -> 1% of each run, Pallas kernels for 0% -> 0%
where the time goes in v1:
time: 301 us; the launch traced here: 300 us
  waiting for transfers between devices  263 us (87%)
  between operations  13.9 us (5%)
  matrix products  9.43 us (3%)
  starting transfers between devices  5.69 us (2%)
  other arithmetic  5.16 us (2%)
  local copies, waits for them, and re-layouts  3.65 us (1%)
    psum x1, waiting for transfers between devices, on_device(): weight_grad = lax.psum(local_term, ('rep', 'blk'))  133 us
    ppermute x4, waiting for transfers between devices, rest_edge(): lax.ppermute(big, 'blk', [(w, w ^ frame_out) for w in range(u_next)])  64.4 us
    all_gather x1, waiting for transfers between devices, on_device(): lax.all_gather(projected, 'blk', axis=0, tiled=True)  42.6 us
    reduce_scatter x1, waiting for transfers between devices, on_device(): lax.psum_scatter(folded.reshape(2 * tile_rows, feat_width).astype(jnp.bfl...  11.8 us
    reduce_scatter x1, waiting for transfers between devices, on_device(): lax.psum_scatter(partial_value.reshape(2 * tile_rows, feat_width).astype(...  10.6 us
  transfers between devices with their start and end apart: 8, of which 8 were waited for; matrix products, arithmetic and copies ran while one was open for 1% of the time, Pallas kernels for 0%

profile of v1, /device:TPU:0, one launch (start us, length us, event | category | flops | bytes accessed | tf_op | source)
XLA Modules:
  0.0 300.3 jit_solution(9487401133238656369)
XLA Ops:
  7.2 0.0 all-gather.2.cloned.1.call-start
  7.2 1.0 copy-done
  8.2 1.8 convolution_convert_fusion.1
  10.0 0.0 all-gather.2.cloned.1.call-update
  10.0 0.0 reduce-scatter.3.cloned.1.call-start
  10.1 0.7 compare_reduce_fusion.1
  10.8 0.1 copy.9
  10.9 1.4 bitcast_multiply_fusion
  12.3 42.6 %all-gather.2.cloned.1.call-done = bf16[2048,512]{1,0:T(8,128)(2,1)} async-done(((bf16[128,512]{1,0:T(8,128)(2,1)}), bf16[2048,512]{1,0:T(8,128)(2,1)}) %all-gather.2.cloned.1.call-update) | async-done | bytes 2097168 | tf_op jit(solution)/shard_map/all_gather | solution.py:53
  54.9 3.0 fusion
  57.9 0.0 reduce-scatter.3.cloned.1.call-update
  58.0 0.0 reduce-scatter.5.cloned.1.call-start
  58.0 10.6 %reduce-scatter.3.cloned.1.call-done = bf16[128,512]{1,0:T(8,128)(2,1)} async-done(((bf16[256,512]{1,0:T(8,128)(2,1)}), bf16[128,512]{1,0:T(8,128)(2,1)}) %reduce-scatter.3.cloned.1.call-update) | async-done | bytes 131088 | tf_op jit(solution)/shard_map/reduce_scatter | solution.py:54
  68.6 1.8 fusion.9
  70.4 1.3 collective-permute-done
  71.7 0.1 maximum_select_fusion.3
  71.8 1.5 collective-permute-start.1
  73.3 6.9 %collective-permute-done.1 = bf16[256,512]{1,0:T(8,128)(2,1)S(1)} collective-permute-done((bf16[256,512]{1,0:T(8,128)(2,1)S(1)}, bf16[256,512]{1,0:T(8,128)(2,1)S(1)}, u32[]{:S(2)}, u32[]{:S(2)}) %collective-permute-start.1) | collective-permute-done | bytes 262176 | tf_op jit(solution)/shard_map/ppermute | solution.py:16
  80.2 0.2 maximum_select_fusion.2
  80.4 1.6 collective-permute-start.2
  82.0 11.6 %collective-permute-done.2 = bf16[512,512]{1,0:T(8,128)(2,1)S(1)} collective-permute-done((bf16[512,512]{1,0:T(8,128)(2,1)S(1)}, bf16[512,512]{1,0:T(8,128)(2,1)S(1)}, u32[]{:S(2)}, u32[]{:S(2)}) %collective-permute-start.2) | collective-permute-done | bytes 524320 | tf_op jit(solution)/shard_map/ppermute | solution.py:16
  93.6 0.5 maximum_select_fusion.1
  94.1 2.5 collective-permute-start.3
  96.5 44.5 %collective-permute-done.3 = bf16[1024,512]{1,0:T(8,128)(2,1)S(1)} collective-permute-done((bf16[1024,512]{1,0:T(8,128)(2,1)S(1)}, bf16[1024,512]{1,0:T(8,128)(2,1)S(1)}, u32[]{:S(2)}, u32[]{:S(2)}) %collective-permute-start.3) | collective-permute-done | bytes 1048608 | tf_op jit(solution)/shard_map/ppermute | solution.py:16
  141.0 0.6 maximum_select_fusion
  141.6 1.4 fusion.1
  143.0 0.0 all-reduce.2.cloned.1.call-start
  143.1 11.8 %reduce-scatter.5.cloned.1.call-done = bf16[128,512]{1,0:T(8,128)(2,1)} async-done(((bf16[256,512]{1,0:T(8,128)(2,1)}), bf16[128,512]{1,0:T(8,128)(2,1)}) %reduce-scatter.5.cloned.1.call-update) | async-done | bytes 131088 | tf_op jit(solution)/shard_map/reduce_scatter | solution.py:66
  154.9 2.3 convolution_bitcast_fusion
  157.2 1.0 convolution_convert_fusion
  158.2 133.1 %all-reduce.2.cloned.1.call-done = f32[512,512]{0,1:T(8,128)} async-done(((f32[512,512]{0,1:T(8,128)}), f32[512,512]{0,1:T(8,128)}) %all-reduce.2.cloned.1.call-update) | async-done | bytes 1048592 | tf_op jit(solution)/shard_map/psum | solution.py:75
  291.3 2.5 copy.10
  (18 shorter events, 0.1 us)
Async XLA Ops:
  7.2 1.0 copy-start
  7.2 47.8 %all-gather.2.cloned.1.call-start = ((), (), s32[]{:S(2)}) async-start(), calls=%async_computation.2 | async-start | bytes 2228224 | tf_op jit(solution)/shard_map/all_gather | solution.py:53
  10.0 58.6 %reduce-scatter.3.cloned.1.call-start = ((), (), s32[]{:S(2)}) async-start(), calls=%async_computation.3 | async-start | bytes 393216 | tf_op jit(solution)/shard_map/reduce_scatter | solution.py:54
  12.3 58.1 %copy-start.1 = (bf16[16,2,128,128]{3,2,1,0:T(8,128)(2,1)}, bf16[16,2,128,128]{3,2,1,0:T(8,128)(2,1)S(1)}, u32[]{:S(2)}) copy-start(bf16[16,2,128,128]{3,2,1,0:T(8,128)(2,1)S(1)} %bitcast_multiply_fusion) | copy-start | bytes 3145732
  12.3 45.7 %copy-start.6 = (s32[128]{0:T(128)S(1)}, s32[128]{0:T(128)}, u32[]{:S(2)}) copy-start(s32[128]{0:T(128)} %param.10) | copy-start | bytes 1540
  12.3 56.3 %copy-start.5 = (bf16[128,512]{1,0:T(8,128)(2,1)S(1)}, bf16[128,512]{1,0:T(8,128)(2,1)}, u32[]{:S(2)}) copy-start(bf16[128,512]{1,0:T(8,128)(2,1)} %param.11) | copy-start | bytes 393220
  58.0 97.0 %reduce-scatter.5.cloned.1.call-start = ((), (), s32[]{:S(2)}) async-start(), calls=%async_computation.4 | async-start | bytes 393216 | tf_op jit(solution)/shard_map/reduce_scatter | solution.py:66
  70.4 1.3 collective-permute-start
  71.8 8.4 %collective-permute-start.1 = (bf16[256,512]{1,0:T(8,128)(2,1)S(1)}, bf16[256,512]{1,0:T(8,128)(2,1)S(1)}, u32[]{:S(2)}, u32[]{:S(2)}) collective-permute-start(bf16[256,512]{1,0:T(8,128)(2,1)S(1)} %maximum_select_fusion.3), channel_id=1, source_target_pairs={{0,2},{1,3},{2,0},{3,1},{4,6},{5,7},{6,4},{7,5},{8,10},{9,11},{10,... | collective-permute-start | bytes 786440 | tf_op jit(solution)/shard_map/ppermute | solution.py:16
  80.4 13.2 %collective-permute-start.2 = (bf16[512,512]{1,0:T(8,128)(2,1)S(1)}, bf16[512,512]{1,0:T(8,128)(2,1)S(1)}, u32[]{:S(2)}, u32[]{:S(2)}) collective-permute-start(bf16[512,512]{1,0:T(8,128)(2,1)S(1)} %maximum_select_fusion.2), channel_id=1, source_target_pairs={{0,4},{1,5},{2,6},{3,7},{4,0},{5,1},{6,2},{7,3},{8,12},{9,13},{10,... | collective-permute-start | bytes 1572872 | tf_op jit(solution)/shard_map/ppermute | solution.py:16
  94.1 46.9 %collective-permute-start.3 = (bf16[1024,512]{1,0:T(8,128)(2,1)S(1)}, bf16[1024,512]{1,0:T(8,128)(2,1)S(1)}, u32[]{:S(2)}, u32[]{:S(2)}) collective-permute-start(bf16[1024,512]{1,0:T(8,128)(2,1)S(1)} %maximum_select_fusion.1), channel_id=1, source_target_pairs={{0,8},{1,9},{2,10},{3,11},{4,12},{5,13},{6,14},{7,15},{8,0},{9,1},... | collective-permute-start | bytes 3145736 | tf_op jit(solution)/shard_map/ppermute | solution.py:16
  96.5 45.1 %copy-start.2 = (bf16[16,2,128,128]{3,2,1,0:T(8,128)(2,1)S(1)}, bf16[16,2,128,128]{3,2,1,0:T(8,128)(2,1)}, u32[]{:S(2)}) copy-start(bf16[16,2,128,128]{3,2,1,0:T(8,128)(2,1)} %copy-done.1) | copy-start | bytes 3145732
  141.6 13.4 %copy-start.3 = (bf16[128,512]{1,0:T(8,128)(2,1)S(1)}, bf16[128,512]{1,0:T(8,128)(2,1)}, u32[]{:S(2)}) copy-start(bf16[128,512]{1,0:T(8,128)(2,1)} %param.6) | copy-start | bytes 393220
  143.0 148.2 %all-reduce.2.cloned.1.call-start = ((), (), s32[]{:S(2)}) async-start(), calls=%async_computation.5 | async-start | bytes 2097152 | tf_op jit(solution)/shard_map/psum | solution.py:75
  154.9 2.3 copy-start.4
Sparse Core Ops, SparseCore 0:
  10.7 44.1 all-gather.1
  58.1 10.4 reduce-scatter.2
  143.2 11.7 reduce-scatter.4
  160.6 130.6 all-reduce.1
